TPU v7x, 32 devices: a whole 2x2x4 slice. The times are simulated.
32 devices in a mesh: mem: 8 (over z, y), lev: 4 (over x, core).
Axes of the slice: x: 2, y: 2, z: 4, core: 2. Of those that a mesh axis runs over, the one named last changes fastest.
Arguments:
- prior_ensemble_stack: float32 [16, 20, 64, 512], P('mem', 'lev'), may hold values from -6 to 6
- vertical_cfl_ratio: float32 [20, 64, 512], P('lev'), may hold values from -0.35 to 0.35
- horizontal_cfl_ratio: float32 [20, 64, 512], P('lev'), may hold values from -0.35 to 0.35
- spreading_coefficient: float32 [20], P('lev'), may hold values from 0.02 to 0.2
- obs_cells: int32 [2, 16], replicated, may hold values from 0 to 32767
- obs_slabs: int32 [2, 16], replicated, may hold values from 0 to 19
- obs_values: float32 [2, 16], replicated, may hold values from -6 to 6
- obs_error: float32 [2, 16], replicated, may hold values from 0.25 to 2
Outputs:
- analysis: float32 [16, 20, 64, 512], P('mem', 'lev')
All inputs are finite; a program needn't handle non-finite values.
Results may differ from a plain program's by a relative error of at most 0.0001.
Values sent between devices are 32-bit elements; how exact they have to be, the bound alone decides.
No kernel may reach another device: no remote copies, remote signals or barrier semaphores. Data moves between devices by JAX's collectives and lax.ppermute only.
A program may use at most 256 MiB of HBM per device.

v0:
```python
import jax
import jax.numpy as jnp
from jax import lax
from jax.sharding import PartitionSpec as P

NX = 512
STEPS = 2
LOC_HALF = 64


def predicted_model_vector(
    ensemble_gridded_values, vertical_cfl_ratio, horizontal_cfl_ratio, spreading_coefficient
):
    diffuse = spreading_coefficient[:, None, None]
    for time_step in range(STEPS):
        widths = [(0, 0)] * (ensemble_gridded_values.ndim - 2) + [(1, 1), (1, 1)]
        padded = jnp.pad(ensemble_gridded_values, widths, mode="edge")
        east_cell = padded[..., 1:-1, 2:]
        west_cell = padded[..., 1:-1, :-2]
        north_cell = padded[..., 2:, 1:-1]
        south_cell = padded[..., :-2, 1:-1]
        ensemble_gridded_values = (
            ensemble_gridded_values
            - 0.5 * vertical_cfl_ratio * (east_cell - west_cell)
            - 0.5 * horizontal_cfl_ratio * (north_cell - south_cell)
            + diffuse
            * (east_cell + west_cell + north_cell + south_cell - 4.0 * ensemble_gridded_values)
        )
    return ensemble_gridded_values


def grid_distance(cells_a, cells_b):
    row_gap = (cells_a[:, None] // NX - cells_b[None, :] // NX).astype(jnp.float32)
    col_gap = (cells_a[:, None] % NX - cells_b[None, :] % NX).astype(jnp.float32)
    return jnp.sqrt(row_gap * row_gap + col_gap * col_gap)


def gaspari_taper(dist):
    scaled = dist / LOC_HALF
    inner_portion = (
        ((-0.25 * scaled + 0.5) * scaled + 0.625) * scaled - 5.0 / 3.0
    ) * scaled * scaled + 1.0
    safe_ratio = jnp.maximum(scaled, 1.0)
    outer_portion = (
        ((((scaled / 12.0 - 0.5) * scaled + 0.625) * scaled + 5.0 / 3.0) * scaled - 5.0) * scaled
        + 4.0
        - 2.0 / (3.0 * safe_ratio)
    )
    return jnp.where(scaled <= 1.0, inner_portion, jnp.where(scaled < 2.0, outer_portion, 0.0))


def obs_space(prior_rows, row_cells, first_row, obs_cell, obs_value, obs_var):
    member_count = prior_rows.shape[1]
    reach_table = gaspari_taper(grid_distance(row_cells, obs_cell))

    def advance_obs(current, position):
        own_row = lax.dynamic_index_in_dim(current, first_row + position, 0, False)
        row_mean = jnp.mean(own_row)
        anomaly = own_row - row_mean
        spread = jnp.sum(anomaly * anomaly) / (member_count - 1) + 1e-06
        error_var = lax.dynamic_index_in_dim(obs_var, position, 0, False)
        seen_value = lax.dynamic_index_in_dim(obs_value, position, 0, False)
        shrink = jnp.sqrt(error_var / (spread + error_var))
        increment = (
            (row_mean * error_var + seen_value * spread) / (spread + error_var)
            - row_mean
            + (shrink - 1.0) * anomaly
        )
        centered = current - jnp.mean(current, axis=1, keepdims=True)
        slopes = jnp.dot(centered, anomaly, precision=lax.Precision.HIGHEST) / (
            (member_count - 1) * spread
        )
        weight = lax.dynamic_index_in_dim(reach_table, position, 1, False)
        current = current + (weight * slopes)[:, None] * increment[None, :]
        return (current, (anomaly, spread, increment))

    positions = jnp.arange(obs_cell.shape[0], dtype=jnp.int32)
    prior_rows, obs_plan = lax.scan(advance_obs, prior_rows, positions)
    return (obs_plan, prior_rows)


def settle(state_rows, obs_plan, cell_loc):
    prior_anoms, spreads, increments = obs_plan
    member_count = state_rows.shape[0]
    centered = state_rows - jnp.mean(state_rows, axis=0, keepdims=True)
    cross_cov = jnp.einsum(
        "km,msc->ksc", prior_anoms, centered, precision=lax.Precision.HIGHEST
    ) / (member_count - 1)
    incr_anom = increments - jnp.mean(increments, axis=1, keepdims=True)
    incr_link = jnp.dot(incr_anom, prior_anoms.T, precision=lax.Precision.HIGHEST) / (
        member_count - 1
    )

    def solve_step(weights, position):
        column = lax.dynamic_index_in_dim(incr_link, position, 1, False)
        summed_total = lax.dynamic_index_in_dim(cross_cov, position, 0, False) + jnp.einsum(
            "j,jsc->sc", column, weights, precision=lax.Precision.HIGHEST
        )
        taper_row = lax.dynamic_index_in_dim(cell_loc, position, 0, False)
        update_row = (
            taper_row[None, :]
            * summed_total
            / lax.dynamic_index_in_dim(spreads, position, 0, False)
        )
        return (lax.dynamic_update_index_in_dim(weights, update_row, position, 0), None)

    positions = jnp.arange(cross_cov.shape[0], dtype=jnp.int32)
    weights, unused = lax.scan(solve_step, jnp.zeros_like(cross_cov), positions)
    return state_rows + jnp.einsum(
        "km,ksc->msc", increments, weights, precision=lax.Precision.HIGHEST
    )


def pick_rows(state_rows, obs_slab, obs_cell, slab_base, cell_base):
    slab_dev = state_rows.shape[1]
    cell_dev = state_rows.shape[2]
    slab_off = obs_slab - slab_base
    cell_off = obs_cell - cell_base
    inside = (slab_off >= 0) & (slab_off < slab_dev) & (cell_off >= 0) & (cell_off < cell_dev)
    taken_rows = state_rows[
        :, jnp.clip(slab_off, 0, slab_dev - 1), jnp.clip(cell_off, 0, cell_dev - 1)
    ]
    return jnp.where(inside[:, None], taken_rows.T, 0.0)


def body(
    prior_ensemble_stack,
    vertical_cfl_ratio,
    horizontal_cfl_ratio,
    spreading_coefficient,
    obs_cells,
    obs_slabs,
    obs_values,
    obs_error,
):
    mem_dev, slab_dev, grid_rows, grid_cols = prior_ensemble_stack.shape
    cell_total = grid_rows * grid_cols
    cell_dev = cell_total // lax.axis_size("mem")
    batch_count = obs_cells.shape[0]
    ensemble_gridded_values = predicted_model_vector(
        prior_ensemble_stack, vertical_cfl_ratio, horizontal_cfl_ratio, spreading_coefficient
    )
    by_cells = ensemble_gridded_values.reshape(mem_dev, slab_dev, cell_total)
    cell_base = lax.axis_index("mem") * cell_dev
    slab_base = lax.axis_index("lev") * slab_dev
    local_cells = cell_base + jnp.arange(cell_dev, dtype=jnp.int32)
    cell_locs = [
        gaspari_taper(grid_distance(obs_cells[batch_no], local_cells))
        for batch_no in range(batch_count)
    ]
    state_rows = lax.all_to_all(by_cells, "mem", split_axis=2, concat_axis=0, tiled=True)
    for batch_no in range(batch_count):
        partial_value = pick_rows(
            state_rows, obs_slabs[batch_no], obs_cells[batch_no], slab_base, cell_base
        )
        prior_rows = lax.psum(partial_value, ("mem", "lev"))
        obs_plan, carried = obs_space(
            prior_rows,
            obs_cells[batch_no],
            0,
            obs_cells[batch_no],
            obs_values[batch_no],
            obs_error[batch_no],
        )
        state_rows = settle(state_rows, obs_plan, cell_locs[batch_no])
    result = lax.all_to_all(state_rows, "mem", split_axis=0, concat_axis=2, tiled=True)
    return result.reshape(prior_ensemble_stack.shape)


def solution(mesh):
    in_specs = (
        P("mem", "lev", None, None),
        P("lev", None, None),
        P("lev", None, None),
        P("lev"),
        P(),
        P(),
        P(),
        P(),
    )
    out_specs = P("mem", "lev", None, None)
    return jax.shard_map(body, mesh=mesh, in_specs=in_specs, out_specs=out_specs, check_vma=False)
```

profile of v0, /device:TPU:0, one launch (start us, length us, event | category | flops | bytes accessed | tf_op | source)
XLA Modules:
  0.0 932.9 jit_solution(16619717677496745712)
XLA Ops:
  1.1 1.5 broadcast_multiply_fusion.2
  2.7 2.2 multiply_add_fusion.5
  5.0 2.2 multiply_add_fusion.4
  7.2 22.3 %copy.76 = f32[2,5,64,512]{1,0,3,2:T(2,128)} copy(f32[2,5,64,512]{3,2,1,0:T(8,128)S(1)} %multiply_add_fusion.4) | data formatting | bytes 2621440 | tf_op jit(solution)/shard_map/reshape | solution.py:143
  29.5 53.2 %reshape.447 = f32[8,1,40960]{2,1,0:T(1,128)} reshape(f32[32768,2,5]{2,1,0:T(2,128)} %bitcast.261) | data formatting | bytes 2621440
  82.7 7.6 all-to-all-start
  92.0 1.6 fusion.55
  93.6 27.9 %all-to-all-done = f32[8,1,40960]{2,1,0:T(1,128)S(1)} async-done(((f32[8,1,40960]{2,1,0:T(1,128)}), f32[8,1,40960]{2,1,0:T(1,128)S(1)}, u32[]{:S(2)}, u32[]{:S(2)}) %all-to-all-start) | async-done | bytes 1310752 | tf_op jit(solution)/shard_map/all_to_all | solution.py:151
  122.0 3.8 reduce.3
  125.8 62.1 %reshape.448 = f32[32768,2,5]{2,1,0:T(2,128)} reshape(f32[8,40960]{1,0:T(8,128)S(1)} %reduce.3) | data formatting | bytes 2621440
  187.9 26.8 %copy.73 = f32[2,5,8,4096]{3,2,0,1:T(8,128)S(1)} copy(f32[2,5,8,4096]{1,0,3,2:T(2,128)} %bitcast.262) | data formatting | bytes 2621440 | tf_op jit(solution)/shard_map/all_to_all | solution.py:151
  216.8 5.5 copy.51
  222.4 1.5 gather_fusion
  223.9 37.7 %psum.14 = f32[16,16]{1,0:T(8,128)S(1)} all-reduce(f32[16,16]{1,0:T(8,128)S(1)} %broadcast_select_fusion.1), channel_id=1, replica_groups=mesh['mem'=8,'lev'=4] {'mem','lev'}, use_global_device_ids=true, to_apply=%region_0.1 | all-reduce | flops 256 | bytes 2048 | tf_op jit(solution)/shard_map/psum | solution.py:156
  261.6 153.8 %while.56 = (s32[]{:T(128)}, f32[16,16]{1,0:T(8,128)S(1)}, f32[16,16]{1,0:T(8,128)S(1)}, f32[16]{0:T(128)S(1)}, f32[16,16]{1,0:T(8,128)S(1)}, /*index=5*/s32[16]...) while((s32[]{:T(128)}, f32[16,16]{1,0:T(8,128)S(1)}, ...), condition=%wide.region_5.6_spmd, body=%wide.region_1.5_spmd.sunk | while | flops 4271 | bytes 5831 | solution.py:78
  415.9 2.2 convolution_multiply_fusion.1
  418.3 118.7 %while.57 = (s32[]{:T(128)}, f32[16,5,4096]{2,1,0:T(8,128)S(1)}, s32[16]{0:T(128)S(1)}, f32[16,4096]{1,0:T(8,128)}, f32[16,5,4096]{2,0,1:T(8,128)}, /*index=5*/f...) while((s32[]{:T(128)}, f32[16,5,4096]{2,1,0:T(8,128)S(1)}, s32[16]{0:T(128)S(1)}, ...), condition=%wide.region_9.10_spmd, body=%wide.region_8.9_spmd.sunk | while | flops 3993605 | bytes 2687667 | solution.py:108
  420.9 1.4 fusion.130
  428.3 1.4 fusion.130
  429.7 1.2 constant_dynamic-slice_fusion.12
  435.7 1.4 fusion.130
  443.1 1.4 fusion.130
  450.5 1.4 fusion.130
  458.0 1.4 fusion.130
  465.4 1.4 fusion.130
  472.8 1.4 fusion.130
  480.2 1.4 fusion.130
  481.7 1.2 constant_dynamic-slice_fusion.12
  487.6 1.4 fusion.130
  489.1 1.2 constant_dynamic-slice_fusion.12
  495.1 1.4 fusion.130
  496.5 1.2 constant_dynamic-slice_fusion.12
  502.5 1.4 fusion.130
  503.9 1.2 constant_dynamic-slice_fusion.12
  509.9 1.4 fusion.130
  517.3 1.4 fusion.130
  524.7 1.4 fusion.130
  532.1 1.4 fusion.130
  537.0 3.3 fusion.97
  540.4 5.5 copy.57
  545.8 1.5 gather_fusion.1
  547.4 41.9 %psum.15 = f32[16,16]{1,0:T(8,128)S(1)} all-reduce(f32[16,16]{1,0:T(8,128)S(1)} %broadcast_select_fusion), channel_id=1, replica_groups=mesh['mem'=8,'lev'=4] {'mem','lev'}, use_global_device_ids=true, to_apply=%region_10.11 | all-reduce | flops 256 | bytes 2048 | tf_op jit(solution)/shard_map/psum | solution.py:156
  589.3 163.1 %while.58 = (s32[]{:T(128)}, f32[16,16]{1,0:T(8,128)S(1)}, f32[16,16]{1,0:T(8,128)S(1)}, f32[16]{0:T(128)S(1)}, f32[16,16]{1,0:T(8,128)S(1)}, /*index=5*/s32[16]...) while((s32[]{:T(128)}, f32[16,16]{1,0:T(8,128)S(1)}, ...), condition=%wide.region_15.16_spmd, body=%wide.region_11.15_spmd.sunk | while | flops 4271 | bytes 5831 | solution.py:78
  753.0 2.2 convolution_multiply_fusion
  755.9 120.0 %while.59 = (s32[]{:T(128)}, f32[16,5,4096]{2,1,0:T(8,128)S(1)}, s32[16]{0:T(128)S(1)}, f32[16,4096]{1,0:T(8,128)}, f32[16,5,4096]{2,0,1:T(8,128)}, /*index=5*/f...) while((s32[]{:T(128)}, f32[16,5,4096]{2,1,0:T(8,128)S(1)}, s32[16]{0:T(128)S(1)}, ...), condition=%wide.region_19.20_spmd, body=%wide.region_18.19_spmd.sunk | while | flops 3993605 | bytes 2687667 | solution.py:108
  758.5 1.4 fusion.140
  766.0 1.4 fusion.140
  773.5 1.4 fusion.140
  781.0 1.4 fusion.140
  788.5 1.4 fusion.140
  796.0 1.4 fusion.140
  803.5 1.4 fusion.140
  811.0 1.4 fusion.140
  818.5 1.4 fusion.140
  826.0 1.4 fusion.140
  833.5 1.4 fusion.140
  841.0 1.4 fusion.140
  848.5 1.4 fusion.140
  856.0 1.4 fusion.140
  863.5 1.4 fusion.140
  871.0 1.4 fusion.140
  875.9 1.9 convolution_add_fusion
  878.6 51.7 %all_to_all.33 = f32[16,5,4096]{2,1,0:T(8,128)S(1)} all-to-all(f32[16,5,4096]{2,1,0:T(8,128)S(1)} %copy.63), channel_id=1, replica_groups=mesh['mem'=8,'lev'=4] {'mem'}, dimensions={0} | all-to-all | bytes 2621440 | tf_op jit(solution)/shard_map/all_to_all | solution.py:166
  931.1 1.3 reshape.421
  (637 shorter events, 262.4 us)
Async XLA Ops:
  1.0 1.7 copy-start.1
  1.0 1.7 copy-start.4
  82.7 7.7 copy-start.2
  82.7 8.7 copy-start.3
  82.7 8.8 copy-start.5
  82.7 8.8 copy-start.6
  82.7 38.8 %all-to-all-start = ((f32[8,1,40960]{2,1,0:T(1,128)}), f32[8,1,40960]{2,1,0:T(1,128)S(1)}, u32[]{:S(2)}, u32[]{:S(2)}) async-start(f32[8,1,40960]{2,1,0:T(1,128)} %reshape.447), calls=%async_computation | async-start | bytes 2621440 | tf_op jit(solution)/shard_map/all_to_all | solution.py:151
  216.8 199.1 %copy-start = (f32[16,5,4096]{2,0,1:T(8,128)}, f32[16,5,4096]{2,0,1:T(8,128)S(1)}, u32[]{:S(2)}) copy-start(f32[16,5,4096]{2,0,1:T(8,128)S(1)} %all_to_all.27) | copy-start | bytes 3932164
  540.3 49.0 %copy-start.7 = (f32[16]{0:T(128)S(1)}, f32[16]{0:T(128)}, u32[]{:S(2)}) copy-start(f32[16]{0:T(128)} %get-tuple-element.825) | copy-start | bytes 196
  540.4 49.0 %copy-start.8 = (f32[16]{0:T(128)S(1)}, f32[16]{0:T(128)}, u32[]{:S(2)}) copy-start(f32[16]{0:T(128)} %get-tuple-element.824) | copy-start | bytes 196
  752.4 0.6 copy-start.9
  755.3 0.7 copy-start.10
where the time goes:
time: 946 us; the launch traced here: 933 us
  local copies, waits for them, and re-layouts  358 us (38%)
  loops' own time  250 us (26%)
  blocking collectives  131 us (14%)
  other arithmetic  83.4 us (9%)
  matrix products  73.5 us (8%)
  waiting for transfers between devices  27.9 us (3%)
    another operation x2, loops' own time, obs_space(): prior_rows, obs_plan = lax.scan(advance_obs, prior_rows, positions)  189 us
    unnamed x24, local copies, waits for them, and re-layouts  116 us
    psum x2, blocking collectives, body(): prior_rows = lax.psum(partial_value, ('mem', 'lev'))  79.6 us
    another operation x2, loops' own time, settle(): weights, unused = lax.scan(solve_step, jnp.zeros_like(cross_cov), positions)  61.9 us
    all_to_all x1, blocking collectives, body(): lax.all_to_all(state_rows, 'mem', split_axis=0, concat_axis=2, tiled=True)  51.7 us
    dot_general x32, matrix products, solve_step(): jnp.einsum('j,jsc->sc', column, weights, precision=lax.Precision.HIGHEST)  46.1 us
    dynamic_slice x64, local copies, waits for them, and re-layouts, obs_space(): prior_rows, obs_plan = lax.scan(advance_obs, prior_rows, positions)  40.3 us
    dynamic_slice x32, local copies, waits for them, and re-layouts, solve_step(): lax.dynamic_index_in_dim(cross_cov, position, 0, False)  36.9 us
  transfers between devices with their start and end apart: 1, of which 1 were waited for; matrix products, arithmetic and copies ran while one was open for 0% of the time, Pallas kernels for 0%

commit v1 on v0

--- a/solution.py
+++ b/solution.py
@@ -148,7 +148,11 @@
         gaspari_taper(grid_distance(obs_cells[batch_no], local_cells))
         for batch_no in range(batch_count)
     ]
-    state_rows = lax.all_to_all(by_cells, "mem", split_axis=2, concat_axis=0, tiled=True)
+    z = lax.psum(1, axis_name="mem")
+    plain = jnp.split(by_cells, z, axis=2)
+    n_now = jnp.stack(plain, axis=0)
+    main = lax.all_to_all(n_now, "mem", split_axis=0, concat_axis=0)
+    state_rows = jnp.concatenate(main, axis=0)
     for batch_no in range(batch_count):
         partial_value = pick_rows(
             state_rows, obs_slabs[batch_no], obs_cells[batch_no], slab_base, cell_base

time: 946 us -> 764 us (0.81)
  local copies, waits for them, and re-layouts: 358 us -> 184 us
    unnamed x24 -> x29, local copies, waits for them, and re-layouts: 116 us -> 5.53 us
    all_to_all x5 -> x1, local copies, waits for them, and re-layouts: 34.7 us -> 1.14 us  [body(): main = lax.all_to_all(n_now, 'mem', split_axis=0, concat_axis=0)]
    reshape x1, local copies, waits for them, and re-layouts: 22.3 us -> 1.11 us  [body(): by_cells = ensemble_gridded_values.reshape(mem_dev, slab_dev, cell_total)]
    dynamic_slice x32, local copies, waits for them, and re-layouts: 36.9 us -> 19.5 us  [solve_step(): lax.dynamic_index_in_dim(cross_cov, position, 0, False)]
where the time goes in v1:
time: 764 us; the launch traced here: 758 us
  loops' own time  253 us (33%)
  local copies, waits for them, and re-layouts  184 us (24%)
  blocking collectives  131 us (17%)
  other arithmetic  81 us (11%)
  matrix products  72.4 us (9%)
  waiting for transfers between devices  28.1 us (4%)
    another operation x2, loops' own time, obs_space(): prior_rows, obs_plan = lax.scan(advance_obs, prior_rows, positions)  189 us
    psum x2, blocking collectives, body(): prior_rows = lax.psum(partial_value, ('mem', 'lev'))  79.7 us
    another operation x2, loops' own time, settle(): weights, unused = lax.scan(solve_step, jnp.zeros_like(cross_cov), positions)  64.8 us
    all_to_all x1, blocking collectives, body(): lax.all_to_all(state_rows, 'mem', split_axis=0, concat_axis=2, tiled=True)  51.7 us
    dot_general x32, matrix products, solve_step(): jnp.einsum('j,jsc->sc', column, weights, precision=lax.Precision.HIGHEST)  46.1 us
    dynamic_slice x64, local copies, waits for them, and re-layouts, obs_space(): prior_rows, obs_plan = lax.scan(advance_obs, prior_rows, positions)  40.5 us
    dynamic_slice x32, local copies, waits for them, and re-layouts, solve_step(): taper_row = lax.dynamic_index_in_dim(cell_loc, position, 0, False)  29.6 us
    all_to_all x1, waiting for transfers between devices, body(): main = lax.all_to_all(n_now, 'mem', split_axis=0, concat_axis=0)  28.1 us
  transfers between devices with their start and end apart: 1, of which 1 were waited for; matrix products, arithmetic and copies ran while one was open for 0% of the time, Pallas kernels for 0%

profile of v1, /device:TPU:0, one launch (start us, length us, event | category | flops | bytes accessed | tf_op | source)
XLA Modules:
  0.0 758.0 jit_solution(1939149092436216332)
XLA Ops:
  1.1 1.5 broadcast_multiply_fusion.2
  2.7 2.2 multiply_add_fusion.5
  5.0 2.2 multiply_add_fusion.4
  13.8 7.5 all-to-all-start
  22.9 1.6 fusion.55
  24.5 28.1 %all-to-all-done = f32[8,2,5,4096]{3,1,2,0:T(2,128)S(1)} async-done(((f32[8,2,5,4096]{3,1,2,0:T(2,128)}), f32[8,2,5,4096]{3,1,2,0:T(2,128)S(1)}, u32[]{:S(2)}, u32[]{:S(2)}) %all-to-all-start) | async-done | bytes 1310752 | tf_op jit(solution)/shard_map/all_to_all | solution.py:154
  53.8 2.2 reshape.424
  56.0 5.5 copy.39
  61.5 1.5 gather_fusion
  63.1 37.9 %psum.14 = f32[16,16]{1,0:T(8,128)S(1)} all-reduce(f32[16,16]{1,0:T(8,128)S(1)} %broadcast_select_fusion.1), channel_id=1, replica_groups=mesh['mem'=8,'lev'=4] {'mem','lev'}, use_global_device_ids=true, to_apply=%region_0.1 | all-reduce | flops 256 | bytes 2048 | tf_op jit(solution)/shard_map/psum | solution.py:160
  101.0 153.8 %while.56 = (s32[]{:T(128)}, f32[16,16]{1,0:T(8,128)S(1)}, f32[16,16]{1,0:T(8,128)S(1)}, f32[16]{0:T(128)S(1)}, f32[16,16]{1,0:T(8,128)S(1)}, /*index=5*/s32[16]...) while((s32[]{:T(128)}, f32[16,16]{1,0:T(8,128)S(1)}, ...), condition=%wide.region_5.6_spmd, body=%wide.region_1.5_spmd.sunk | while | flops 4271 | bytes 5831 | solution.py:78
  255.8 1.2 convolution_multiply_fusion.1
  257.2 106.8 %while.57 = (s32[]{:T(128)}, f32[16,5,4096]{2,1,0:T(8,128)S(1)}, s32[16]{0:T(128)S(1)}, f32[16,4096]{1,0:T(8,128)}, f32[16,5,4096]{2,0,1:T(8,128)S(1)}, /*index=...) while((s32[]{:T(128)}, f32[16,5,4096]{2,1,0:T(8,128)S(1)}, s32[16]{0:T(128)S(1)}, ...), condition=%wide.region_9.10_spmd, body=%wide.region_8.9_spmd.sunk | while | flops 3993605 | bytes 2687667 | solution.py:108
  260.0 1.4 fusion.138
  266.7 1.4 fusion.138
  273.3 1.4 fusion.138
  280.0 1.4 fusion.138
  286.7 1.4 fusion.138
  293.4 1.4 fusion.138
  300.0 1.4 fusion.138
  306.7 1.4 fusion.138
  313.4 1.4 fusion.138
  320.0 1.4 fusion.138
  326.7 1.4 fusion.138
  333.4 1.4 fusion.138
  340.1 1.4 fusion.138
  346.7 1.4 fusion.138
  353.4 1.4 fusion.138
  360.1 1.4 fusion.138
  364.0 3.3 fusion.105
  367.3 5.5 copy.45
  372.8 1.5 gather_fusion.1
  374.4 41.8 %psum.15 = f32[16,16]{1,0:T(8,128)S(1)} all-reduce(f32[16,16]{1,0:T(8,128)S(1)} %broadcast_select_fusion), channel_id=1, replica_groups=mesh['mem'=8,'lev'=4] {'mem','lev'}, use_global_device_ids=true, to_apply=%region_10.11 | all-reduce | flops 256 | bytes 2048 | tf_op jit(solution)/shard_map/psum | solution.py:160
  416.3 163.1 %while.58 = (s32[]{:T(128)}, f32[16,16]{1,0:T(8,128)S(1)}, f32[16,16]{1,0:T(8,128)S(1)}, f32[16]{0:T(128)S(1)}, f32[16,16]{1,0:T(8,128)S(1)}, /*index=5*/s32[16]...) while((s32[]{:T(128)}, f32[16,16]{1,0:T(8,128)S(1)}, ...), condition=%wide.region_15.16_spmd, body=%wide.region_11.15_spmd.sunk | while | flops 4271 | bytes 5831 | solution.py:78
  579.9 2.2 convolution_multiply_fusion
  582.8 118.7 %while.59 = (s32[]{:T(128)}, f32[16,5,4096]{2,1,0:T(8,128)S(1)}, s32[16]{0:T(128)S(1)}, f32[16,4096]{1,0:T(8,128)}, f32[16,5,4096]{2,0,1:T(8,128)}, /*index=5*/f...) while((s32[]{:T(128)}, f32[16,5,4096]{2,1,0:T(8,128)S(1)}, s32[16]{0:T(128)S(1)}, ...), condition=%wide.region_19.20_spmd, body=%wide.region_18.19_spmd.sunk | while | flops 3993605 | bytes 2687667 | solution.py:108
  585.3 1.4 fusion.148
  586.8 1.2 constant_dynamic-slice_fusion.14
  592.7 1.4 fusion.148
  594.2 1.2 constant_dynamic-slice_fusion.14
  600.2 1.4 fusion.148
  607.6 1.4 fusion.148
  615.0 1.4 fusion.148
  616.4 1.2 constant_dynamic-slice_fusion.14
  622.4 1.4 fusion.148
  623.9 1.2 constant_dynamic-slice_fusion.14
  629.8 1.4 fusion.148
  631.3 1.2 constant_dynamic-slice_fusion.14
  637.3 1.4 fusion.148
  638.7 1.2 constant_dynamic-slice_fusion.14
  644.7 1.4 fusion.148
  646.1 1.2 constant_dynamic-slice_fusion.14
  652.1 1.4 fusion.148
  653.6 1.2 constant_dynamic-slice_fusion.14
  659.5 1.4 fusion.148
  661.0 1.2 constant_dynamic-slice_fusion.14
  666.9 1.4 fusion.148
  674.4 1.4 fusion.148
  681.8 1.4 fusion.148
  689.2 1.4 fusion.148
  696.6 1.4 fusion.148
  701.5 1.9 convolution_add_fusion
  704.2 51.7 %all_to_all.20 = f32[16,5,4096]{2,1,0:T(8,128)S(1)} all-to-all(f32[16,5,4096]{2,1,0:T(8,128)S(1)} %copy.51), channel_id=1, replica_groups=mesh['mem'=8,'lev'=4] {'mem'}, dimensions={0} | all-to-all | bytes 2621440 | tf_op jit(solution)/shard_map/all_to_all | solution.py:170
  756.7 1.3 reshape.425
  (641 shorter events, 247.4 us)
Async XLA Ops:
  1.0 1.7 copy-start.1
  1.0 1.7 copy-start.4
  13.8 7.5 copy-start.2
  13.8 8.5 %copy-start.3 = (s32[2,16]{1,0:T(2,128)S(1)}, s32[2,16]{1,0:T(2,128)}, u32[]{:S(2)}) copy-start(s32[2,16]{1,0:T(2,128)} %param.21) | copy-start | bytes 388
  13.8 8.6 %copy-start.5 = (f32[2,16]{1,0:T(2,128)S(1)}, f32[2,16]{1,0:T(2,128)}, u32[]{:S(2)}) copy-start(f32[2,16]{1,0:T(2,128)} %param.22) | copy-start | bytes 388
  13.8 8.6 %copy-start.6 = (f32[2,16]{1,0:T(2,128)S(1)}, f32[2,16]{1,0:T(2,128)}, u32[]{:S(2)}) copy-start(f32[2,16]{1,0:T(2,128)} %param.23) | copy-start | bytes 388
  13.8 38.8 %all-to-all-start = ((f32[8,2,5,4096]{3,1,2,0:T(2,128)}), f32[8,2,5,4096]{3,1,2,0:T(2,128)S(1)}, u32[]{:S(2)}, u32[]{:S(2)}) async-start(f32[8,2,5,4096]{3,1,2,0:T(2,128)} %fusion.58), calls=%async_computation | async-start | bytes 2621440 | tf_op jit(solution)/shard_map/all_to_all | solution.py:154
  56.0 199.9 %copy-start = (f32[16,5,4096]{2,0,1:T(8,128)}, f32[16,5,4096]{2,0,1:T(8,128)S(1)}, u32[]{:S(2)}) copy-start(f32[16,5,4096]{2,0,1:T(8,128)S(1)} %reshape.424) | copy-start | bytes 3932164
  367.3 48.9 %copy-start.7 = (f32[16]{0:T(128)S(1)}, f32[16]{0:T(128)}, u32[]{:S(2)}) copy-start(f32[16]{0:T(128)} %get-tuple-element.793) | copy-start | bytes 196
  367.3 48.9 %copy-start.8 = (f32[16]{0:T(128)S(1)}, f32[16]{0:T(128)}, u32[]{:S(2)}) copy-start(f32[16]{0:T(128)} %get-tuple-element.792) | copy-start | bytes 196
  579.4 0.5 copy-start.9
  582.2 0.6 copy-start.10
